TPU v7x, 256 devices: a whole 4x4x8 slice. The times are simulated.
256 devices in a mesh: pole: 8 (over x_hi, y), row: 32 (over x_lo, z, core).
Axes of the slice: x: 4 (x_hi: 2, x_lo: 2; x = x_hi * 2 + x_lo), y: 4, z: 8, core: 2. Of those that a mesh axis runs over, the one named last changes fastest.
Arguments:
- basis: bfloat16 [131072, 128], P('row'), may hold values from -24 to 24
- inverses: bfloat16 [8, 256, 512, 512], P('pole', 'row'), may hold values from -1.5 to 1.5
- lower: bfloat16 [256, 512, 512], P('row'), may hold values from -0.03955078 to 0.03955078
- upper: bfloat16 [256, 512, 512], P('row'), may hold values from -0.03955078 to 0.03955078
- pole_weights: float32 [8], P('pole'), may hold values from 0.5 to 1.5
Outputs:
- new_basis: float32 [131072, 128], P(('row', 'pole'))
All inputs are finite; a program needn't handle non-finite values.
Results may differ from a plain program's by a relative error of at most 0.003.
Values may be sent and summed in bfloat16 or wider, within the bound.
No kernel may reach another device: no remote copies, remote signals or barrier semaphores. Data moves between devices by JAX's collectives and lax.ppermute only.
A program may use at most 64 MiB of HBM per device.

v0:
```python
import jax
import jax.numpy as jnp
from jax import lax
from jax.sharding import PartitionSpec as P

SWEEPS = 4


def padded_2(value, sides, width):
    for axis, dim in sides:
        peers, length = (lax.axis_size(axis), value.shape[dim])
        up = [(i, (i + 1) % peers) for i in range(peers - 1)]
        down = [(j, i) for i, j in up]
        last = lax.slice_in_dim(value, length - width, length, axis=dim)
        initial = lax.slice_in_dim(value, 0, width, axis=dim)
        before = lax.ppermute(last, axis, up)
        after = lax.ppermute(initial, axis, down)
        value = jnp.concatenate([before, value, after], axis=dim)
    return value


def sent_to_all(value, axis):
    copies = jnp.broadcast_to(value, (lax.axis_size(axis), *value.shape))
    return lax.all_to_all(copies, axis, split_axis=0, concat_axis=0, tiled=True)


def of_everyone(value, axis):
    return sent_to_all(value, axis).sum(axis=0)


def shards(basis, inverses, lower, upper, pole_weights):
    rows, width = basis.shape
    count = inverses.shape[1]
    size = inverses.shape[-1]
    inverse = inverses[0]
    blocks = basis.reshape(count, size, width)
    state = jnp.einsum("bij,bjk->bik", inverse, blocks, preferred_element_type=jnp.float32).astype(
        jnp.bfloat16
    )
    for sweep in range(SWEEPS):
        padded = padded_2(state.reshape(rows, width), (("row", 0),), size)
        padded = padded.reshape(count + 2, size, width)
        rhs = blocks.astype(jnp.float32)
        rhs = rhs + jnp.einsum(
            "bij,bjk->bik", lower, padded[:-2], preferred_element_type=jnp.float32
        )
        rhs = rhs + jnp.einsum(
            "bij,bjk->bik", upper, padded[2:], preferred_element_type=jnp.float32
        )
        state = jnp.einsum(
            "bij,bjk->bik", inverse, rhs.astype(jnp.bfloat16), preferred_element_type=jnp.float32
        ).astype(jnp.bfloat16)
    weighted = pole_weights[0] * state.reshape(rows, width).astype(jnp.float32)
    total_rows = rows * lax.axis_size("row")
    filtered = lax.psum(weighted, "pole")
    share = rows // lax.axis_size("pole")
    mine = lax.dynamic_slice_in_dim(filtered, lax.axis_index("pole") * share, share, 0)
    partial_gram = jnp.dot(filtered.T, filtered)
    gram = of_everyone(partial_gram, "row")
    gram = gram / total_rows
    factor = jnp.linalg.cholesky(gram)
    solved = jax.scipy.linalg.solve_triangular(factor, mine.T, lower=True)
    return solved.T


def solution(mesh):
    return jax.shard_map(
        shards,
        mesh=mesh,
        in_specs=(
            P("row", None),
            P("pole", "row", None, None),
            P("row", None, None),
            P("row", None, None),
            P("pole"),
        ),
        out_specs=P(("row", "pole"), None),
        check_vma=False,
    )
```

profile of v0, /device:TPU:32, one launch (start us, length us, event | category | flops | bytes accessed | tf_op | source)
XLA Modules:
  0.0 303.1 jit_solution(8116113924164155831)
XLA Ops:
  6.5 0.0 all-reduce.2.cloned.1.call-start
  6.5 0.0 copy-start
  6.5 3.8 %fusion.18 = bf16[8,512,128]{2,1,0:T(8,128)(2,1)S(1)} fusion(bf16[8,512,128]{2,1,0:T(8,128)(2,1)} %bitcast.142, bf16[1,8,512,512]{3,2,1,0:T(8,128)(2,1)} %param.6), kind=kOutput, calls=%fused_computation.23 | convolution fusion | flops 537395200 | bytes 6291456 | tf_op jit(solution)/shard_map/bij,bjk->bik/dot_general | solution.py:37
  10.4 1.9 collective-permute-start
  12.3 3.6 %collective-permute-start.1 = (bf16[512,128]{1,0:T(8,128)(2,1)S(1)}, bf16[512,128]{1,0:T(8,128)(2,1)}, u32[]{:S(2)}, u32[]{:S(2)}) collective-permute-start(bf16[512,128]{1,0:T(8,128)(2,1)S(1)} %get-tuple-element.19), channel_id=1, source_target_pairs={{1,0},{2,1},{3,2},{4,3},{5,4},{6,5},{7,6},{8,7},{9,8},{10,9},{11,1... | collective-permute-start | bytes 393224 | tf_op jit(solution)/shard_map/ppermute | solution.py:17
  16.0 0.0 copy-done
  16.0 0.5 copy.38
  16.5 0.2 collective-permute-done
  16.7 1.8 collective-permute-done.1
  18.5 2.0 pad_maximum_fusion.6
  20.5 3.7 %fusion.50 = f32[8,128,512]{2,1,0:T(8,128)S(1)} fusion(bf16[8,512,128]{2,1,0:T(8,128)(2,1)S(1)} %bitcast.131, bf16[8,512,512]{2,1,0:T(8,128)(2,1)} %param.7), kind=kOutput, calls=%fused_computation.59 | convolution fusion | flops 536870912 | bytes 7340032 | tf_op jit(solution)/shard_map/bij,bjk->bik/dot_general | solution.py:44
  24.2 7.7 %fusion.41 = bf16[8,512,128]{1,2,0:T(8,128)(2,1)} fusion(bf16[1,8,512,512]{3,2,1,0:T(8,128)(2,1)} %param.6, bf16[8,512,128]{1,2,0:T(8,128)(2,1)S(1)} %copy.38, f32[8,128,512]{2,1,0:T(8,128)S(1)} %fusion.50, bf16[8,512,128]{2,1,0:T(8,128)(2,1)} %bitcast.138, bf16[8,512,512]{2,1,0:T(8,128)(2,1)} %param.8), kind=kOutput, calls=%fused_computation.30 | convolution fusion | flops 1076363264 | bytes 13631488 | tf_op jit(solution)/shard_map/bij,bjk->bik/dot_general | solution.py:50
  31.9 1.0 slice_bitcast_fusion.4
  32.8 4.2 %collective-permute-start.2 = (bf16[512,128]{0,1:T(8,128)(2,1)S(1)}, bf16[512,128]{0,1:T(8,128)(2,1)S(1)}, u32[]{:S(2)}, u32[]{:S(2)}) collective-permute-start(bf16[512,128]{0,1:T(8,128)(2,1)S(1)} %get-tuple-element.16), channel_id=1, source_target_pairs={{0,1},{1,2},{2,3},{3,4},{4,5},{5,6},{6,7},{7,8},{8,9},{9,10},{10,1... | collective-permute-start | bytes 393224 | tf_op jit(solution)/shard_map/ppermute | solution.py:16
  37.0 1.9 collective-permute-start.3
  39.0 1.6 copy.41
  40.6 0.0 collective-permute-done.2
  40.6 0.1 copy.42
  40.7 0.7 collective-permute-done.3
  41.5 0.1 copy.44
  41.6 1.1 pad_maximum_fusion.4
  42.7 3.7 %fusion.51 = f32[8,128,512]{2,1,0:T(8,128)S(1)} fusion(bf16[8,512,128]{2,1,0:T(8,128)(2,1)S(1)} %bitcast.132, bf16[8,512,512]{2,1,0:T(8,128)(2,1)} %param.7), kind=kOutput, calls=%fused_computation.60 | convolution fusion | flops 536870912 | bytes 7340032 | tf_op jit(solution)/shard_map/bij,bjk->bik/dot_general | solution.py:44
  46.4 7.7 %fusion.38 = bf16[8,512,128]{1,2,0:T(8,128)(2,1)} fusion(bf16[1,8,512,512]{3,2,1,0:T(8,128)(2,1)} %param.6, bf16[8,512,128]{1,2,0:T(8,128)(2,1)S(1)} %copy.38, f32[8,128,512]{2,1,0:T(8,128)S(1)} %fusion.51, bf16[8,512,128]{2,1,0:T(8,128)(2,1)} %bitcast.139, bf16[8,512,512]{2,1,0:T(8,128)(2,1)} %param.8), kind=kOutput, calls=%fused_computation.29 | convolution fusion | flops 1076363264 | bytes 13631488 | tf_op jit(solution)/shard_map/bij,bjk->bik/dot_general | solution.py:50
  54.1 1.0 slice_bitcast_fusion.2
  55.0 4.1 %collective-permute-start.4 = (bf16[512,128]{0,1:T(8,128)(2,1)S(1)}, bf16[512,128]{0,1:T(8,128)(2,1)S(1)}, u32[]{:S(2)}, u32[]{:S(2)}) collective-permute-start(bf16[512,128]{0,1:T(8,128)(2,1)S(1)} %get-tuple-element.12), channel_id=1, source_target_pairs={{0,1},{1,2},{2,3},{3,4},{4,5},{5,6},{6,7},{7,8},{8,9},{9,10},{10,1... | collective-permute-start | bytes 393224 | tf_op jit(solution)/shard_map/ppermute | solution.py:16
  59.1 1.9 collective-permute-start.5
  61.0 1.6 copy.46
  62.7 0.0 collective-permute-done.4
  62.7 0.1 copy.47
  62.8 0.7 collective-permute-done.5
  63.5 0.1 copy.49
  63.7 1.1 pad_maximum_fusion.2
  64.8 3.7 %fusion.52 = f32[8,128,512]{2,1,0:T(8,128)S(1)} fusion(bf16[8,512,128]{2,1,0:T(8,128)(2,1)S(1)} %bitcast.133, bf16[8,512,512]{2,1,0:T(8,128)(2,1)} %param.7), kind=kOutput, calls=%fused_computation.61 | convolution fusion | flops 536870912 | bytes 7340032 | tf_op jit(solution)/shard_map/bij,bjk->bik/dot_general | solution.py:44
  68.5 7.7 %fusion.35 = bf16[8,512,128]{1,2,0:T(8,128)(2,1)} fusion(bf16[1,8,512,512]{3,2,1,0:T(8,128)(2,1)} %param.6, bf16[8,512,128]{1,2,0:T(8,128)(2,1)S(1)} %copy.38, f32[8,128,512]{2,1,0:T(8,128)S(1)} %fusion.52, bf16[8,512,128]{2,1,0:T(8,128)(2,1)} %bitcast.140, bf16[8,512,512]{2,1,0:T(8,128)(2,1)} %param.8), kind=kOutput, calls=%fused_computation.28 | convolution fusion | flops 1076363264 | bytes 13631488 | tf_op jit(solution)/shard_map/bij,bjk->bik/dot_general | solution.py:50
  76.1 1.0 slice_bitcast_fusion
  77.1 6.5 %collective-permute-start.6 = (bf16[512,128]{0,1:T(8,128)(2,1)S(1)}, bf16[512,128]{0,1:T(8,128)(2,1)S(1)}, u32[]{:S(2)}, u32[]{:S(2)}) collective-permute-start(bf16[512,128]{0,1:T(8,128)(2,1)S(1)} %get-tuple-element.8), channel_id=1, source_target_pairs={{0,1},{1,2},{2,3},{3,4},{4,5},{5,6},{6,7},{7,8},{8,9},{9,10},{10,1... | collective-permute-start | bytes 393224 | tf_op jit(solution)/shard_map/ppermute | solution.py:16
  83.6 2.1 collective-permute-start.7
  86.4 1.6 copy.51
  88.0 0.0 collective-permute-done.6
  88.0 0.1 copy.52
  88.1 0.0 collective-permute-done.7
  88.2 0.1 copy.54
  88.3 1.1 pad_maximum_fusion
  89.4 3.7 %fusion.53 = f32[8,128,512]{2,1,0:T(8,128)S(1)} fusion(bf16[8,512,128]{2,1,0:T(8,128)(2,1)S(1)} %bitcast.134, bf16[8,512,512]{2,1,0:T(8,128)(2,1)} %param.7), kind=kOutput, calls=%fused_computation.62 | convolution fusion | flops 536870912 | bytes 7340032 | tf_op jit(solution)/shard_map/bij,bjk->bik/dot_general | solution.py:44
  93.1 8.0 %multiply_bitcast_fusion = f32[8,512,128]{1,2,0:T(8,128)} fusion(bf16[1,8,512,512]{3,2,1,0:T(8,128)(2,1)} %param.6, bf16[8,512,128]{1,2,0:T(8,128)(2,1)S(1)} %copy.38, f32[8,128,512]{2,1,0:T(8,128)S(1)} %fusion.53, bf16[8,512,128]{2,1,0:T(8,128)(2,1)} %bitcast.130, bf16[8,512,512]{2,1,0:T(8,128)(2,1)} %param.8, f32[]{:T(128)} %bitcast.128), kind=kOutput, calls=%fused_computation.22 | convolution fusion | flops 1077411840 | bytes 14680068 | tf_op jit(solution)/shard_map/bij,bjk->bik/dot_general | solution.py:50
  101.1 2.9 copy.56
  104.0 0.0 all-reduce.2.cloned.1.call-update
  104.0 103.8 %all-reduce.2.cloned.1.call-done = f32[4096,128]{1,0:T(8,128)} async-done(((f32[4096,128]{1,0:T(8,128)}), f32[4096,128]{1,0:T(8,128)}) %all-reduce.2.cloned.1.call-update) | async-done | bytes 2097168 | tf_op jit(solution)/shard_map/psum | solution.py:55
  207.8 2.7 fusion.54
  210.5 1.6 broadcast_in_dim.5
  212.1 7.6 %all-to-all-start = ((f32[32,128,128]{2,1,0:T(8,128)}), f32[32,128,128]{2,1,0:T(8,128)S(1)}, u32[]{:S(2)}, u32[]{:S(2)}) async-start(f32[32,128,128]{2,1,0:T(8,128)} %broadcast_in_dim.5), calls=%async_computation | async-start | bytes 4194304 | tf_op jit(solution)/shard_map/all_to_all | solution.py:24
  219.7 51.5 %all-to-all-done = f32[32,128,128]{2,1,0:T(8,128)S(1)} async-done(((f32[32,128,128]{2,1,0:T(8,128)}), f32[32,128,128]{2,1,0:T(8,128)S(1)}, u32[]{:S(2)}, u32[]{:S(2)}) %all-to-all-start) | async-done | bytes 2097184 | tf_op jit(solution)/shard_map/all_to_all | solution.py:24
  271.2 0.1 reduce_sum.11
  271.3 0.1 copy.57
  271.4 11.7 %cholesky.16 = f32[128,128]{1,0:T(8,128)S(1)} custom-call(f32[128,128]{1,0:T(8,128)S(1)} %fusion.48), custom_call_target="Cholesky" | custom-call | tf_op jit(solution)/shard_map/jit(cholesky)/cholesky | solution.py:61
  283.2 0.6 compare_reduce_fusion
  283.8 0.7 fusion.46
  284.5 9.8 %custom-call.7 = f32[1,128,128]{1,2,0:T(8,128)S(1)} custom-call(f32[1,128,128]{2,1,0:T(8,128)S(1)} %fusion.46), custom_call_target="InvertDiagBlocksLowerTriangular" | custom-call | tf_op jit(solution)/shard_map/jit(_solve_triangular)/triangular_solve | solution.py:62
  294.3 2.0 fusion.44
  (3 shorter events, 0.1 us)
Async XLA Ops:
  6.5 201.3 %all-reduce.2.cloned.1.call-start = ((), (), s32[]{:S(2)}) async-start(), calls=%async_computation.1 | async-start | bytes 4194304 | tf_op jit(solution)/shard_map/psum | solution.py:55
  6.5 9.4 %copy-start = (bf16[4096,128]{1,0:T(8,128)(2,1)S(1)}, bf16[4096,128]{1,0:T(8,128)(2,1)}, u32[]{:S(2)}) copy-start(bf16[4096,128]{1,0:T(8,128)(2,1)} %param.5) | copy-start | bytes 3145732
  10.4 6.3 %collective-permute-start = (bf16[512,128]{1,0:T(8,128)(2,1)S(1)}, bf16[512,128]{1,0:T(8,128)(2,1)S(1)}, u32[]{:S(2)}, u32[]{:S(2)}) collective-permute-start(bf16[512,128]{1,0:T(8,128)(2,1)S(1)} %get-tuple-element.20), channel_id=1, source_target_pairs={{0,1},{1,2},{2,3},{3,4},{4,5},{5,6},{6,7},{7,8},{8,9},{9,10},{10,1... | collective-permute-start | bytes 393224 | tf_op jit(solution)/shard_map/ppermute | solution.py:16
  12.3 6.2 %collective-permute-start.1 = (bf16[512,128]{1,0:T(8,128)(2,1)S(1)}, bf16[512,128]{1,0:T(8,128)(2,1)}, u32[]{:S(2)}, u32[]{:S(2)}) collective-permute-start(bf16[512,128]{1,0:T(8,128)(2,1)S(1)} %get-tuple-element.19), channel_id=1, source_target_pairs={{1,0},{2,1},{3,2},{4,3},{5,4},{6,5},{7,6},{8,7},{9,8},{10,9},{11,1... | collective-permute-start | bytes 393224 | tf_op jit(solution)/shard_map/ppermute | solution.py:17
  32.8 7.7 %collective-permute-start.2 = (bf16[512,128]{0,1:T(8,128)(2,1)S(1)}, bf16[512,128]{0,1:T(8,128)(2,1)S(1)}, u32[]{:S(2)}, u32[]{:S(2)}) collective-permute-start(bf16[512,128]{0,1:T(8,128)(2,1)S(1)} %get-tuple-element.16), channel_id=1, source_target_pairs={{0,1},{1,2},{2,3},{3,4},{4,5},{5,6},{6,7},{7,8},{8,9},{9,10},{10,1... | collective-permute-start | bytes 393224 | tf_op jit(solution)/shard_map/ppermute | solution.py:16
  37.0 4.4 %collective-permute-start.3 = (bf16[512,128]{0,1:T(8,128)(2,1)S(1)}, bf16[512,128]{0,1:T(8,128)(2,1)S(1)}, u32[]{:S(2)}, u32[]{:S(2)}) collective-permute-start(bf16[512,128]{0,1:T(8,128)(2,1)S(1)} %get-tuple-element.15), channel_id=1, source_target_pairs={{1,0},{2,1},{3,2},{4,3},{5,4},{6,5},{7,6},{8,7},{9,8},{10,9},{11,1... | collective-permute-start | bytes 393224 | tf_op jit(solution)/shard_map/ppermute | solution.py:17
  55.0 7.6 %collective-permute-start.4 = (bf16[512,128]{0,1:T(8,128)(2,1)S(1)}, bf16[512,128]{0,1:T(8,128)(2,1)S(1)}, u32[]{:S(2)}, u32[]{:S(2)}) collective-permute-start(bf16[512,128]{0,1:T(8,128)(2,1)S(1)} %get-tuple-element.12), channel_id=1, source_target_pairs={{0,1},{1,2},{2,3},{3,4},{4,5},{5,6},{6,7},{7,8},{8,9},{9,10},{10,1... | collective-permute-start | bytes 393224 | tf_op jit(solution)/shard_map/ppermute | solution.py:16
  59.1 4.4 %collective-permute-start.5 = (bf16[512,128]{0,1:T(8,128)(2,1)S(1)}, bf16[512,128]{0,1:T(8,128)(2,1)S(1)}, u32[]{:S(2)}, u32[]{:S(2)}) collective-permute-start(bf16[512,128]{0,1:T(8,128)(2,1)S(1)} %get-tuple-element.11), channel_id=1, source_target_pairs={{1,0},{2,1},{3,2},{4,3},{5,4},{6,5},{7,6},{8,7},{9,8},{10,9},{11,1... | collective-permute-start | bytes 393224 | tf_op jit(solution)/shard_map/ppermute | solution.py:17
  77.1 10.9 %collective-permute-start.6 = (bf16[512,128]{0,1:T(8,128)(2,1)S(1)}, bf16[512,128]{0,1:T(8,128)(2,1)S(1)}, u32[]{:S(2)}, u32[]{:S(2)}) collective-permute-start(bf16[512,128]{0,1:T(8,128)(2,1)S(1)} %get-tuple-element.8), channel_id=1, source_target_pairs={{0,1},{1,2},{2,3},{3,4},{4,5},{5,6},{6,7},{7,8},{8,9},{9,10},{10,1... | collective-permute-start | bytes 393224 | tf_op jit(solution)/shard_map/ppermute | solution.py:16
  83.6 4.5 %collective-permute-start.7 = (bf16[512,128]{0,1:T(8,128)(2,1)S(1)}, bf16[512,128]{0,1:T(8,128)(2,1)S(1)}, u32[]{:S(2)}, u32[]{:S(2)}) collective-permute-start(bf16[512,128]{0,1:T(8,128)(2,1)S(1)} %get-tuple-element.7), channel_id=1, source_target_pairs={{1,0},{2,1},{3,2},{4,3},{5,4},{6,5},{7,6},{8,7},{9,8},{10,9},{11,1... | collective-permute-start | bytes 393224 | tf_op jit(solution)/shard_map/ppermute | solution.py:17
  212.1 59.1 %all-to-all-start = ((f32[32,128,128]{2,1,0:T(8,128)}), f32[32,128,128]{2,1,0:T(8,128)S(1)}, u32[]{:S(2)}, u32[]{:S(2)}) async-start(f32[32,128,128]{2,1,0:T(8,128)} %broadcast_in_dim.5), calls=%async_computation | async-start | bytes 4194304 | tf_op jit(solution)/shard_map/all_to_all | solution.py:24
Sparse Core Ops, SparseCore 0:
  104.1 103.6 all-reduce.1
where the time goes:
time: 304 us; the launch traced here: 303 us
  waiting for transfers between devices  159 us (52%)
  matrix products  54.3 us (18%)
  starting transfers between devices  33.9 us (11%)
  other arithmetic  28.4 us (9%)
  between operations  14.3 us (5%)
  local copies, waits for them, and re-layouts  13.6 us (4%)
    psum x1, waiting for transfers between devices, shards(): filtered = lax.psum(weighted, 'pole')  104 us
    all_to_all x1, waiting for transfers between devices, sent_to_all(): return lax.all_to_all(copies, axis, split_axis=0, concat_axis=0, tiled=True)  51.5 us
    dot_general x4, matrix products, shards(): jnp.einsum('bij,bjk->bik', inverse, rhs.astype(jnp.bfloat16), preferred_e...  31 us
    ppermute x4, starting transfers between devices, padded_2(): before = lax.ppermute(last, axis, up)  16.6 us
    dot_general x4, matrix products, shards(): jnp.einsum('bij,bjk->bik', lower, padded[:-2], preferred_element_type=jnp...  14.8 us
    another operation x3, other arithmetic, shards(): factor = jnp.linalg.cholesky(gram)  12.4 us
    another operation x2, other arithmetic, shards(): solved = jax.scipy.linalg.solve_triangular(factor, mine.T, lower=True)  10.5 us
    ppermute x4, starting transfers between devices, padded_2(): after = lax.ppermute(initial, axis, down)  9.59 us
  transfers between devices with their start and end apart: 10, of which 6 were waited for; matrix products, arithmetic and copies ran while one was open for 2% of the time, Pallas kernels for 0%

commit v1 on v0

--- a/solution.py
+++ b/solution.py
@@ -52,7 +52,7 @@
         ).astype(jnp.bfloat16)
     weighted = pole_weights[0] * state.reshape(rows, width).astype(jnp.float32)
     total_rows = rows * lax.axis_size("row")
-    filtered = lax.psum(weighted, "pole")
+    filtered = jnp.sum(lax.all_gather(weighted, "pole"), axis=0)
     share = rows // lax.axis_size("pole")
     mine = lax.dynamic_slice_in_dim(filtered, lax.axis_index("pole") * share, share, 0)
     partial_gram = jnp.dot(filtered.T, filtered)

time: 304 us -> 399 us (1.31)
  waiting for transfers between devices: 159 us -> 249 us
  other arithmetic: 28.4 us -> 36.8 us
    all_gather x0 -> x1, waiting for transfers between devices: none -> 194 us  [shards(): filtered = jnp.sum(lax.all_gather(weighted, 'pole'), axis=0)]
    psum x1 -> x0, waiting for transfers between devices: 104 us -> none  [shards(): filtered = lax.psum(weighted, 'pole')]
    reduce_sum x0 -> x1, other arithmetic: none -> 6.81 us  [shards(): filtered = jnp.sum(lax.all_gather(weighted, 'pole'), axis=0)]
  transfers between devices with their start and end apart: 10 -> 10, of which waited for: 6 -> 6; matrix products, arithmetic and copies ran while one was open for 2% -> 1% of each run, Pallas kernels for 0% -> 0%
where the time goes in v1:
time: 399 us
  waiting for transfers between devices  249 us (62%)
  matrix products  51.1 us (13%)
  other arithmetic  36.8 us (9%)
  starting transfers between devices  33.9 us (8%)
  between operations  14.3 us (4%)
  local copies, waits for them, and re-layouts  13.6 us (3%)
    all_gather x1, waiting for transfers between devices, shards(): filtered = jnp.sum(lax.all_gather(weighted, 'pole'), axis=0)  194 us
    all_to_all x1, waiting for transfers between devices, sent_to_all(): return lax.all_to_all(copies, axis, split_axis=0, concat_axis=0, tiled=True)  51.5 us
    dot_general x4, matrix products, shards(): jnp.einsum('bij,bjk->bik', inverse, rhs.astype(jnp.bfloat16), preferred_e...  31 us
    ppermute x4, starting transfers between devices, padded_2(): before = lax.ppermute(last, axis, up)  16.6 us
    dot_general x4, matrix products, shards(): jnp.einsum('bij,bjk->bik', lower, padded[:-2], preferred_element_type=jnp...  14.8 us
    another operation x3, other arithmetic, shards(): factor = jnp.linalg.cholesky(gram)  12.4 us
    another operation x2, other arithmetic, shards(): solved = jax.scipy.linalg.solve_triangular(factor, mine.T, lower=True)  10.5 us
    ppermute x4, starting transfers between devices, padded_2(): after = lax.ppermute(initial, axis, down)  9.59 us
  transfers between devices with their start and end apart: 10, of which 6 were waited for; matrix products, arithmetic and copies ran while one was open for 1% of the time, Pallas kernels for 0%

profile of v1, /device:TPU:32, one launch (start us, length us, event | category | flops | bytes accessed | tf_op | source)
XLA Modules:
  0.0 398.6 jit_solution(8185266180664427449)
XLA Ops:
  6.5 0.0 all-gather.2.cloned.1.call-start
  6.5 0.0 copy-start
  6.5 3.8 fusion.18
  10.4 1.9 collective-permute-start
  12.3 3.6 collective-permute-start.1
  16.0 0.0 copy-done
  16.0 0.5 copy.58
  16.5 0.2 collective-permute-done
  16.7 1.8 collective-permute-done.1
  18.5 2.0 pad_maximum_fusion.6
  20.5 3.7 fusion.50
  24.2 7.7 %fusion.41 = bf16[8,512,128]{1,2,0:T(8,128)(2,1)} fusion(bf16[1,8,512,512]{3,2,1,0:T(8,128)(2,1)} %param.6, bf16[8,512,128]{1,2,0:T(8,128)(2,1)S(1)} %copy.58, f32[8,128,512]{2,1,0:T(8,128)S(1)} %fusion.50, bf16[8,512,128]{2,1,0:T(8,128)(2,1)} %bitcast.138, bf16[8,512,512]{2,1,0:T(8,128)(2,1)} %param.8), kind=kOutput, calls=%fused_computation.30 | convolution fusion | flops 1076363264 | bytes 13631488 | tf_op jit(solution)/shard_map/bij,bjk->bik/dot_general | solution.py:50
  31.9 1.0 slice_bitcast_fusion.4
  32.8 4.2 %collective-permute-start.2 = (bf16[512,128]{0,1:T(8,128)(2,1)S(1)}, bf16[512,128]{0,1:T(8,128)(2,1)S(1)}, u32[]{:S(2)}, u32[]{:S(2)}) collective-permute-start(bf16[512,128]{0,1:T(8,128)(2,1)S(1)} %get-tuple-element.16), channel_id=1, source_target_pairs={{0,1},{1,2},{2,3},{3,4},{4,5},{5,6},{6,7},{7,8},{8,9},{9,10},{10,1... | collective-permute-start | bytes 393224 | tf_op jit(solution)/shard_map/ppermute | solution.py:16
  37.0 1.9 collective-permute-start.3
  39.0 1.6 copy.61
  40.6 0.0 collective-permute-done.2
  40.6 0.1 copy.62
  40.7 0.7 collective-permute-done.3
  41.5 0.1 copy.64
  41.6 1.1 pad_maximum_fusion.4
  42.7 3.7 fusion.51
  46.4 7.7 %fusion.38 = bf16[8,512,128]{1,2,0:T(8,128)(2,1)} fusion(bf16[1,8,512,512]{3,2,1,0:T(8,128)(2,1)} %param.6, bf16[8,512,128]{1,2,0:T(8,128)(2,1)S(1)} %copy.58, f32[8,128,512]{2,1,0:T(8,128)S(1)} %fusion.51, bf16[8,512,128]{2,1,0:T(8,128)(2,1)} %bitcast.139, bf16[8,512,512]{2,1,0:T(8,128)(2,1)} %param.8), kind=kOutput, calls=%fused_computation.29 | convolution fusion | flops 1076363264 | bytes 13631488 | tf_op jit(solution)/shard_map/bij,bjk->bik/dot_general | solution.py:50
  54.1 1.0 slice_bitcast_fusion.2
  55.0 4.1 %collective-permute-start.4 = (bf16[512,128]{0,1:T(8,128)(2,1)S(1)}, bf16[512,128]{0,1:T(8,128)(2,1)S(1)}, u32[]{:S(2)}, u32[]{:S(2)}) collective-permute-start(bf16[512,128]{0,1:T(8,128)(2,1)S(1)} %get-tuple-element.12), channel_id=1, source_target_pairs={{0,1},{1,2},{2,3},{3,4},{4,5},{5,6},{6,7},{7,8},{8,9},{9,10},{10,1... | collective-permute-start | bytes 393224 | tf_op jit(solution)/shard_map/ppermute | solution.py:16
  59.1 1.9 collective-permute-start.5
  61.0 1.6 copy.66
  62.7 0.0 collective-permute-done.4
  62.7 0.1 copy.67
  62.8 0.7 collective-permute-done.5
  63.5 0.1 copy.69
  63.7 1.1 pad_maximum_fusion.2
  64.8 3.7 fusion.52
  68.5 7.7 %fusion.35 = bf16[8,512,128]{1,2,0:T(8,128)(2,1)} fusion(bf16[1,8,512,512]{3,2,1,0:T(8,128)(2,1)} %param.6, bf16[8,512,128]{1,2,0:T(8,128)(2,1)S(1)} %copy.58, f32[8,128,512]{2,1,0:T(8,128)S(1)} %fusion.52, bf16[8,512,128]{2,1,0:T(8,128)(2,1)} %bitcast.140, bf16[8,512,512]{2,1,0:T(8,128)(2,1)} %param.8), kind=kOutput, calls=%fused_computation.28 | convolution fusion | flops 1076363264 | bytes 13631488 | tf_op jit(solution)/shard_map/bij,bjk->bik/dot_general | solution.py:50
  76.1 1.0 slice_bitcast_fusion
  77.1 6.5 %collective-permute-start.6 = (bf16[512,128]{0,1:T(8,128)(2,1)S(1)}, bf16[512,128]{0,1:T(8,128)(2,1)S(1)}, u32[]{:S(2)}, u32[]{:S(2)}) collective-permute-start(bf16[512,128]{0,1:T(8,128)(2,1)S(1)} %get-tuple-element.8), channel_id=1, source_target_pairs={{0,1},{1,2},{2,3},{3,4},{4,5},{5,6},{6,7},{7,8},{8,9},{9,10},{10,1... | collective-permute-start | bytes 393224 | tf_op jit(solution)/shard_map/ppermute | solution.py:16
  83.6 2.1 collective-permute-start.7
  86.4 1.6 copy.71
  88.0 0.0 collective-permute-done.6
  88.0 0.1 copy.72
  88.1 0.0 collective-permute-done.7
  88.2 0.1 copy.74
  88.3 1.1 pad_maximum_fusion
  89.4 3.7 fusion.53
  93.1 8.0 %multiply_bitcast_fusion = f32[8,512,128]{1,2,0:T(8,128)} fusion(bf16[1,8,512,512]{3,2,1,0:T(8,128)(2,1)} %param.6, bf16[8,512,128]{1,2,0:T(8,128)(2,1)S(1)} %copy.58, f32[8,128,512]{2,1,0:T(8,128)S(1)} %fusion.53, bf16[8,512,128]{2,1,0:T(8,128)(2,1)} %bitcast.130, bf16[8,512,512]{2,1,0:T(8,128)(2,1)} %param.8, f32[]{:T(128)} %bitcast.128), kind=kOutput, calls=%fused_computation.22 | convolution fusion | flops 1077411840 | bytes 14680068 | tf_op jit(solution)/shard_map/bij,bjk->bik/dot_general | solution.py:50
  101.1 2.9 copy.76
  104.0 0.0 all-gather.2.cloned.1.call-update
  104.0 193.9 %all-gather.2.cloned.1.call-done = f32[8,4096,128]{2,1,0:T(8,128)} async-done(((f32[1,4096,128]{2,1,0:T(8,128)}), f32[8,4096,128]{2,1,0:T(8,128)}) %all-gather.2.cloned.1.call-update) | async-done | bytes 16777232 | tf_op jit(solution)/shard_map/all_gather | solution.py:55
  297.9 6.8 %reduce_sum.20 = f32[4096,128]{1,0:T(8,128)S(1)} reduce(f32[8,4096,128]{2,1,0:T(8,128)} %all-gather.2.cloned.1.call-done, f32[]{:T(128)} %constant.50.clone.1), dimensions={0}, to_apply=%region_0.0 | reduce | flops 3670016 | bytes 18874372 | tf_op jit(solution)/shard_map/reduce_sum | solution.py:55
  304.8 0.5 fusion.54
  305.2 1.6 broadcast_in_dim.5
  306.8 7.7 %all-to-all-start = ((f32[32,128,128]{2,1,0:T(8,128)}), f32[32,128,128]{2,1,0:T(8,128)}, u32[]{:S(2)}, u32[]{:S(2)}) async-start(f32[32,128,128]{2,1,0:T(8,128)} %broadcast_in_dim.5), calls=%async_computation | async-start | bytes 4194304 | tf_op jit(solution)/shard_map/all_to_all | solution.py:24
  314.5 51.5 %all-to-all-done = f32[32,128,128]{2,1,0:T(8,128)} async-done(((f32[32,128,128]{2,1,0:T(8,128)}), f32[32,128,128]{2,1,0:T(8,128)}, u32[]{:S(2)}, u32[]{:S(2)}) %all-to-all-start) | async-done | bytes 2097184 | tf_op jit(solution)/shard_map/all_to_all | solution.py:24
  366.0 1.7 reduce_sum.21
  367.7 0.1 copy.77
  367.8 11.7 %cholesky.16 = f32[128,128]{1,0:T(8,128)S(1)} custom-call(f32[128,128]{1,0:T(8,128)S(1)} %fusion.48), custom_call_target="Cholesky" | custom-call | tf_op jit(solution)/shard_map/jit(cholesky)/cholesky | solution.py:61
  379.6 0.6 compare_reduce_fusion
  380.2 0.7 fusion.46
  380.9 9.8 %custom-call.7 = f32[1,128,128]{1,2,0:T(8,128)S(1)} custom-call(f32[1,128,128]{2,1,0:T(8,128)S(1)} %fusion.46), custom_call_target="InvertDiagBlocksLowerTriangular" | custom-call | tf_op jit(solution)/shard_map/jit(_solve_triangular)/triangular_solve | solution.py:62
  390.7 1.1 fusion.44
  (3 shorter events, 0.1 us)
Async XLA Ops:
  6.5 291.4 %all-gather.2.cloned.1.call-start = ((), (), s32[]{:S(2)}) async-start(), calls=%async_computation.1 | async-start | bytes 18874368 | tf_op jit(solution)/shard_map/all_gather | solution.py:55
  6.5 9.4 %copy-start = (bf16[4096,128]{1,0:T(8,128)(2,1)S(1)}, bf16[4096,128]{1,0:T(8,128)(2,1)}, u32[]{:S(2)}) copy-start(bf16[4096,128]{1,0:T(8,128)(2,1)} %param.5) | copy-start | bytes 3145732
  10.4 6.3 %collective-permute-start = (bf16[512,128]{1,0:T(8,128)(2,1)S(1)}, bf16[512,128]{1,0:T(8,128)(2,1)S(1)}, u32[]{:S(2)}, u32[]{:S(2)}) collective-permute-start(bf16[512,128]{1,0:T(8,128)(2,1)S(1)} %get-tuple-element.20), channel_id=1, source_target_pairs={{0,1},{1,2},{2,3},{3,4},{4,5},{5,6},{6,7},{7,8},{8,9},{9,10},{10,1... | collective-permute-start | bytes 393224 | tf_op jit(solution)/shard_map/ppermute | solution.py:16
  12.3 6.2 %collective-permute-start.1 = (bf16[512,128]{1,0:T(8,128)(2,1)S(1)}, bf16[512,128]{1,0:T(8,128)(2,1)}, u32[]{:S(2)}, u32[]{:S(2)}) collective-permute-start(bf16[512,128]{1,0:T(8,128)(2,1)S(1)} %get-tuple-element.19), channel_id=1, source_target_pairs={{1,0},{2,1},{3,2},{4,3},{5,4},{6,5},{7,6},{8,7},{9,8},{10,9},{11,1... | collective-permute-start | bytes 393224 | tf_op jit(solution)/shard_map/ppermute | solution.py:17
  32.8 7.7 %collective-permute-start.2 = (bf16[512,128]{0,1:T(8,128)(2,1)S(1)}, bf16[512,128]{0,1:T(8,128)(2,1)S(1)}, u32[]{:S(2)}, u32[]{:S(2)}) collective-permute-start(bf16[512,128]{0,1:T(8,128)(2,1)S(1)} %get-tuple-element.16), channel_id=1, source_target_pairs={{0,1},{1,2},{2,3},{3,4},{4,5},{5,6},{6,7},{7,8},{8,9},{9,10},{10,1... | collective-permute-start | bytes 393224 | tf_op jit(solution)/shard_map/ppermute | solution.py:16
  37.0 4.4 %collective-permute-start.3 = (bf16[512,128]{0,1:T(8,128)(2,1)S(1)}, bf16[512,128]{0,1:T(8,128)(2,1)S(1)}, u32[]{:S(2)}, u32[]{:S(2)}) collective-permute-start(bf16[512,128]{0,1:T(8,128)(2,1)S(1)} %get-tuple-element.15), channel_id=1, source_target_pairs={{1,0},{2,1},{3,2},{4,3},{5,4},{6,5},{7,6},{8,7},{9,8},{10,9},{11,1... | collective-permute-start | bytes 393224 | tf_op jit(solution)/shard_map/ppermute | solution.py:17
  55.0 7.6 %collective-permute-start.4 = (bf16[512,128]{0,1:T(8,128)(2,1)S(1)}, bf16[512,128]{0,1:T(8,128)(2,1)S(1)}, u32[]{:S(2)}, u32[]{:S(2)}) collective-permute-start(bf16[512,128]{0,1:T(8,128)(2,1)S(1)} %get-tuple-element.12), channel_id=1, source_target_pairs={{0,1},{1,2},{2,3},{3,4},{4,5},{5,6},{6,7},{7,8},{8,9},{9,10},{10,1... | collective-permute-start | bytes 393224 | tf_op jit(solution)/shard_map/ppermute | solution.py:16
  59.1 4.4 %collective-permute-start.5 = (bf16[512,128]{0,1:T(8,128)(2,1)S(1)}, bf16[512,128]{0,1:T(8,128)(2,1)S(1)}, u32[]{:S(2)}, u32[]{:S(2)}) collective-permute-start(bf16[512,128]{0,1:T(8,128)(2,1)S(1)} %get-tuple-element.11), channel_id=1, source_target_pairs={{1,0},{2,1},{3,2},{4,3},{5,4},{6,5},{7,6},{8,7},{9,8},{10,9},{11,1... | collective-permute-start | bytes 393224 | tf_op jit(solution)/shard_map/ppermute | solution.py:17
  77.1 10.9 %collective-permute-start.6 = (bf16[512,128]{0,1:T(8,128)(2,1)S(1)}, bf16[512,128]{0,1:T(8,128)(2,1)S(1)}, u32[]{:S(2)}, u32[]{:S(2)}) collective-permute-start(bf16[512,128]{0,1:T(8,128)(2,1)S(1)} %get-tuple-element.8), channel_id=1, source_target_pairs={{0,1},{1,2},{2,3},{3,4},{4,5},{5,6},{6,7},{7,8},{8,9},{9,10},{10,1... | collective-permute-start | bytes 393224 | tf_op jit(solution)/shard_map/ppermute | solution.py:16
  83.6 4.5 %collective-permute-start.7 = (bf16[512,128]{0,1:T(8,128)(2,1)S(1)}, bf16[512,128]{0,1:T(8,128)(2,1)S(1)}, u32[]{:S(2)}, u32[]{:S(2)}) collective-permute-start(bf16[512,128]{0,1:T(8,128)(2,1)S(1)} %get-tuple-element.7), channel_id=1, source_target_pairs={{1,0},{2,1},{3,2},{4,3},{5,4},{6,5},{7,6},{8,7},{9,8},{10,9},{11,1... | collective-permute-start | bytes 393224 | tf_op jit(solution)/shard_map/ppermute | solution.py:17
  306.8 59.2 %all-to-all-start = ((f32[32,128,128]{2,1,0:T(8,128)}), f32[32,128,128]{2,1,0:T(8,128)}, u32[]{:S(2)}, u32[]{:S(2)}) async-start(f32[32,128,128]{2,1,0:T(8,128)} %broadcast_in_dim.5), calls=%async_computation | async-start | bytes 4194304 | tf_op jit(solution)/shard_map/all_to_all | solution.py:24
Sparse Core Ops, SparseCore 0:
  104.1 193.7 all-gather.1
